TPU v7x, 32 devices: a whole 2x2x4 slice. The times are simulated.
32 devices in a mesh: tm: 8 (over z, x), rows: 4 (over y, core).
Axes of the slice: x: 2, y: 2, z: 4, core: 2. Of those that a mesh axis runs over, the one named last changes fastest.
Arguments:
- latents: bfloat16 [32, 16, 32, 256], P('tm', 'rows'), may hold values from -6 to 6
- frame_gaps: float32 [32], P('tm'), may hold values from 0.5 to 250
- decay_rates: float32 [2, 256], replicated, may hold values from 0.0011 to 0.05
- input_kernel: bfloat16 [2, 3, 3, 256, 256], replicated, may hold values from -0.125 to 0.125
- output_kernel: bfloat16 [2, 3, 3, 256, 256], replicated, may hold values from -0.125 to 0.125
- feedthrough: float32 [2, 256], replicated, may hold values from -1 to 1
Outputs:
- encoded: bfloat16 [32, 16, 32, 256], P('tm', 'rows')
All inputs are finite; a program needn't handle non-finite values.
Results may differ from a plain program's by a relative error of at most 0.012.
Values may be sent and summed in bfloat16 or wider, within the bound.
A program may use at most 64 MiB of HBM per device.

v0:
```python
import jax
import jax.numpy as jnp
from jax import lax
from jax.sharding import PartitionSpec as P

STACK_COUNT = 2


def extended(cells, sides, width):
    for axis, dim in sides:
        count = lax.axis_size(axis)
        ends = count - 1
        head = lax.slice_in_dim(cells, 0, width, axis=dim)
        tail = lax.slice_in_dim(cells, cells.shape[dim] - width, cells.shape[dim], axis=dim)
        cells = jnp.concatenate(
            [
                lax.ppermute(tail, axis, [(i, (i + 1) % count) for i in range(ends)]),
                cells,
                lax.ppermute(head, axis, [((i + 1) % count, i) for i in range(ends)]),
            ],
            axis=dim,
        )
    return cells


def convolve(inputs, kernel):
    frames, vertical_extent, columns, channels = inputs.shape
    padded = extended(inputs, (("rows", 1),), 1)
    padded = jnp.pad(padded, ((0, 0), (0, 0), (1, 1), (0, 0)))
    summed = jnp.zeros((frames * vertical_extent * columns, kernel.shape[-1]), jnp.float32)
    for row_tap in range(3):
        for col_tap in range(3):
            window = padded[
                :, row_tap : row_tap + vertical_extent, col_tap : col_tap + columns, :
            ].reshape(-1, channels)
            summed = summed + jnp.dot(
                window, kernel[row_tap, col_tap], preferred_element_type=jnp.float32
            )
    return summed.reshape(frames, vertical_extent, columns, -1)


def local_states(driving, decays):

    def advance(carried, pieces):
        driven, factor = pieces
        carried = factor * carried + jnp.sqrt(1.0 - factor * factor) * driven
        return (carried, carried)

    initial = jnp.zeros(driving.shape[1:], jnp.float32)
    _, states = lax.scan(advance, initial, (driving, decays))
    return states


def combine(earlier, latter):
    return (earlier[0] * latter[0], latter[0] * earlier[1] + latter[1])


def carried_in(segment_attenuation, block_state):
    band, columns, channels = block_state.shape
    flat_state = block_state.reshape(1, band * columns, channels)
    flattened_decay = segment_attenuation.reshape(1, 1, channels)
    spread_decay, spread_state = (
        lax.all_to_all(flattened_decay, "tm", split_axis=2, concat_axis=0, tiled=True),
        lax.all_to_all(flat_state, "tm", split_axis=2, concat_axis=0, tiled=True),
    )
    _, inclusive = lax.associative_scan(combine, (spread_decay, spread_state), axis=0)
    exclusive = jnp.concatenate([jnp.zeros_like(inclusive[:1]), inclusive[:-1]], axis=0)
    returned = lax.all_to_all(
        exclusive.astype(jnp.bfloat16), "tm", split_axis=0, concat_axis=2, tiled=True
    ).astype(exclusive.dtype)
    incoming = returned.reshape(band, columns, channels)
    return incoming


def per_device(latents, frame_gaps, decay_rates, input_kernel, output_kernel, feedthrough):
    inputs = latents
    for layer_index in range(STACK_COUNT):
        layer_rates = decay_rates[layer_index]
        decays = jnp.exp(-frame_gaps[:, None] * layer_rates[None, :])
        driving = convolve(inputs, input_kernel[layer_index])
        states = local_states(driving, decays)
        cumulative = jnp.cumprod(decays, axis=0)
        incoming = carried_in(cumulative[-1], states[-1])
        states = states + cumulative[:, None, None, :] * incoming[None]
        rounded_states = states.astype(jnp.bfloat16)
        premix = convolve(rounded_states, output_kernel[layer_index]) + feedthrough[
            layer_index
        ] * inputs.astype(jnp.float32)
        inputs = jax.nn.gelu(premix, approximate=True).astype(jnp.bfloat16)
    return inputs


def solution(mesh):
    in_specs = (P("tm", "rows", None, None), P("tm"), P(), P(), P(), P())
    out_specs = P("tm", "rows", None, None)
    return jax.shard_map(
        per_device, mesh=mesh, in_specs=in_specs, out_specs=out_specs, check_vma=False
    )
```

profile of v0, /device:TPU:1, one launch (start us, length us, event | category | flops | bytes accessed | tf_op | source)
XLA Modules:
  0.0 124.7 jit_solution(17457823050170934931)
XLA Ops:
  0.0 0.9 fusion.48
  0.9 4.5 %collective-permute-start = (bf16[4,1,32,256]{3,2,1,0:T(8,128)(2,1)S(1)}, bf16[4,1,32,256]{3,2,1,0:T(8,128)(2,1)S(1)}, u32[]{:S(2)}, u32[]{:S(2)}) collective-permute-start(bf16[4,1,32,256]{3,2,1,0:T(8,128)(2,1)S(1)} %get-tuple-element.163), channel_id=1, source_target_pairs={{0,1},{1,2},{2,3},{4,5},{5,6},{6,7},{8,9},{9,10},{10,11},{12,13},{... | collective-permute-start | bytes 196616 | tf_op jit(solution)/shard_map/ppermute | solution.py:17
  5.4 1.9 %collective-permute-start.1 = (bf16[4,1,32,256]{3,2,1,0:T(8,128)(2,1)S(1)}, bf16[4,1,32,256]{3,2,1,0:T(8,128)(2,1)S(1)}, u32[]{:S(2)}, u32[]{:S(2)}) collective-permute-start(bf16[4,1,32,256]{3,2,1,0:T(8,128)(2,1)S(1)} %get-tuple-element.164), channel_id=1, source_target_pairs={{1,0},{2,1},{3,2},{5,4},{6,5},{7,6},{9,8},{10,9},{11,10},{13,12},{... | collective-permute-start | bytes 196616 | tf_op jit(solution)/shard_map/ppermute | solution.py:19
  7.3 0.8 fusion.52
  8.1 0.7 neg.5
  8.9 0.8 copy.39
  9.7 5.5 %all-to-all-start.1 = ((f32[1,1,256]{1,0,2:T(1,128)}), f32[1,1,256]{1,0,2:T(1,128)S(1)}, u32[]{:S(2)}, u32[]{:S(2)}) async-start(f32[1,1,256]{1,0,2:T(1,128)} %copy.39), calls=%async_computation.1 | async-start | bytes 262144 | tf_op jit(solution)/shard_map/all_to_all | solution.py:63
  15.2 1.8 %slice_bitcast_fusion.1 = (bf16[3,3,256,256]{3,2,1,0:T(8,128)(2,1)S(1)}, bf16[3,3,256,256]{3,2,1,0:T(8,128)(2,1)S(1)}) fusion(bf16[2,3,3,256,256]{4,3,2,1,0:T(8,128)(2,1)} %param.13), kind=kLoop, calls=%fused_computation.47 | loop fusion | bytes 4718592 | tf_op jit(solution)/shard_map/squeeze | solution.py:80
  17.1 4.4 %all-to-all-done.1 = f32[1,1,256]{1,0,2:T(1,128)S(1)} async-done(((f32[1,1,256]{1,0,2:T(1,128)}), f32[1,1,256]{1,0,2:T(1,128)S(1)}, u32[]{:S(2)}, u32[]{:S(2)}) %all-to-all-start.1) | async-done | bytes 1056 | tf_op jit(solution)/shard_map/all_to_all | solution.py:63
  21.4 1.0 reduce
  22.9 0.3 fusion.44
  25.1 1.0 fusion.5
  26.2 4.1 %while.26 = (s32[]{:T(128)}, f32[4,32,256]{2,1,0:T(8,128)S(1)}, f32[4,4,32,256]{3,2,1,0:T(8,128)S(1)}, f32[4,256]{1,0:T(4,128)S(1)}, f32[4,4,32,256]{3,2,1,0:T(8,128)}, /*index=5*/s32[]{:T(128)}, s32[]{:T(128)}) while((s32[]{:T(128)}, f32[4,32,256]{2,1,0:T(8,128)S(1)}, f32[4,4,32,256]{3,2,1,0:T(8,128)S(1)}, ...), condition=%wide.region_1.2_spmd.clone, body=%wide.region_0.1_spmd.clone.sunk | while | flops 131587 | bytes 530527 | solution.py:50
  26.2 1.0 bitcast_dynamic-update-slice_fusion.4
  27.2 1.0 bitcast_dynamic-update-slice_fusion.4
  28.3 1.0 bitcast_dynamic-update-slice_fusion.4
  29.3 1.0 bitcast_dynamic-update-slice_fusion.4
  30.3 0.8 copy.37
  31.0 3.4 %all-to-all-start = ((f32[1,128,256]{1,0,2:T(1,128)}), f32[1,128,256]{1,0,2:T(1,128)S(1)}, u32[]{:S(2)}, u32[]{:S(2)}) async-start(f32[1,128,256]{1,0,2:T(1,128)} %copy.37), calls=%async_computation | async-start | bytes 262144 | tf_op jit(solution)/shard_map/all_to_all | solution.py:64
  34.5 7.2 %all-to-all-done = f32[1,128,256]{1,0,2:T(1,128)S(1)} async-done(((f32[1,128,256]{1,0,2:T(1,128)}), f32[1,128,256]{1,0,2:T(1,128)S(1)}, u32[]{:S(2)}, u32[]{:S(2)}) %all-to-all-start) | async-done | bytes 131104 | tf_op jit(solution)/shard_map/all_to_all | solution.py:64
  42.3 0.6 concatenate.59
  42.9 3.4 %all-to-all-start.2 = ((bf16[8,128,32]{1,2,0:T(8,128)(2,1)}), bf16[8,128,32]{1,2,0:T(8,128)(2,1)S(1)}, u32[]{:S(2)}, u32[]{:S(2)}) async-start(bf16[8,128,32]{1,2,0:T(8,128)(2,1)} %concatenate.59), calls=%async_computation.2 | async-start | bytes 131072 | tf_op jit(solution)/shard_map/all_to_all | solution.py:68
  46.3 2.8 %slice_bitcast_fusion = (bf16[3,3,256,256]{3,2,1,0:T(8,128)(2,1)S(1)}, bf16[3,3,256,256]{3,2,1,0:T(8,128)(2,1)}) fusion(bf16[2,3,3,256,256]{4,3,2,1,0:T(8,128)(2,1)} %param.14), kind=kLoop, calls=%fused_computation.46 | loop fusion | bytes 4718592 | tf_op jit(solution)/shard_map/squeeze | solution.py:86
  49.2 2.8 %all-to-all-done.2 = bf16[8,128,32]{1,2,0:T(8,128)(2,1)S(1)} async-done(((bf16[8,128,32]{1,2,0:T(8,128)(2,1)}), bf16[8,128,32]{1,2,0:T(8,128)(2,1)S(1)}, u32[]{:S(2)}, u32[]{:S(2)}) %all-to-all-start.2) | async-done | bytes 65568 | tf_op jit(solution)/shard_map/all_to_all | solution.py:68
  52.0 1.1 reshape.228
  53.1 1.2 copy.45
  54.4 6.2 %collective-permute-start.2 = (bf16[4,1,32,256]{3,2,1,0:T(8,128)(2,1)S(1)}, bf16[4,1,32,256]{3,2,1,0:T(8,128)(2,1)S(1)}, u32[]{:S(2)}, u32[]{:S(2)}) collective-permute-start(bf16[4,1,32,256]{3,2,1,0:T(8,128)(2,1)S(1)} %get-tuple-element.159), channel_id=1, source_target_pairs={{0,1},{1,2},{2,3},{4,5},{5,6},{6,7},{8,9},{9,10},{10,11},{12,13},{... | collective-permute-start | bytes 196616 | tf_op jit(solution)/shard_map/ppermute | solution.py:17
  60.7 1.9 %collective-permute-start.3 = (bf16[4,1,32,256]{3,2,1,0:T(8,128)(2,1)S(1)}, bf16[4,1,32,256]{3,2,1,0:T(8,128)(2,1)S(1)}, u32[]{:S(2)}, u32[]{:S(2)}) collective-permute-start(bf16[4,1,32,256]{3,2,1,0:T(8,128)(2,1)S(1)} %get-tuple-element.160), channel_id=1, source_target_pairs={{1,0},{2,1},{3,2},{5,4},{6,5},{7,6},{9,8},{10,9},{11,10},{13,12},{... | collective-permute-start | bytes 196616 | tf_op jit(solution)/shard_map/ppermute | solution.py:19
  62.7 3.6 %collective-permute-done.3 = bf16[4,1,32,256]{3,2,1,0:T(8,128)(2,1)S(1)} collective-permute-done((bf16[4,1,32,256]{3,2,1,0:T(8,128)(2,1)S(1)}, bf16[4,1,32,256]{3,2,1,0:T(8,128)(2,1)S(1)}, u32[]{:S(2)}, u32[]{:S(2)}) %collective-permute-start.3) | collective-permute-done | bytes 65568 | tf_op jit(solution)/shard_map/ppermute | solution.py:19
  66.5 0.3 fusion.43
  66.8 1.0 copy-done.1
  70.1 1.9 %collective-permute-start.4 = (bf16[4,1,32,256]{3,2,1,0:T(8,128)(2,1)S(1)}, bf16[4,1,32,256]{3,2,1,0:T(8,128)(2,1)S(1)}, u32[]{:S(2)}, u32[]{:S(2)}) collective-permute-start(bf16[4,1,32,256]{3,2,1,0:T(8,128)(2,1)S(1)} %get-tuple-element.155), channel_id=1, source_target_pairs={{0,1},{1,2},{2,3},{4,5},{5,6},{6,7},{8,9},{9,10},{10,11},{12,13},{... | collective-permute-start | bytes 196616 | tf_op jit(solution)/shard_map/ppermute | solution.py:17
  72.0 2.4 %collective-permute-start.5 = (bf16[4,1,32,256]{3,2,1,0:T(8,128)(2,1)S(1)}, bf16[4,1,32,256]{3,2,1,0:T(8,128)(2,1)S(1)}, u32[]{:S(2)}, u32[]{:S(2)}) collective-permute-start(bf16[4,1,32,256]{3,2,1,0:T(8,128)(2,1)S(1)} %get-tuple-element.156), channel_id=1, source_target_pairs={{1,0},{2,1},{3,2},{5,4},{6,5},{7,6},{9,8},{10,9},{11,10},{13,12},{... | collective-permute-start | bytes 196616 | tf_op jit(solution)/shard_map/ppermute | solution.py:19
  74.5 0.8 copy.43
  75.3 3.4 %all-to-all-start.4 = ((f32[1,1,256]{1,0,2:T(1,128)}), f32[1,1,256]{1,0,2:T(1,128)S(1)}, u32[]{:S(2)}, u32[]{:S(2)}) async-start(f32[1,1,256]{1,0,2:T(1,128)} %copy.43), calls=%async_computation.4 | async-start | bytes 262144 | tf_op jit(solution)/shard_map/all_to_all | solution.py:63
  78.7 7.0 %all-to-all-done.4 = f32[1,1,256]{1,0,2:T(1,128)S(1)} async-done(((f32[1,1,256]{1,0,2:T(1,128)}), f32[1,1,256]{1,0,2:T(1,128)S(1)}, u32[]{:S(2)}, u32[]{:S(2)}) %all-to-all-start.4) | async-done | bytes 1056 | tf_op jit(solution)/shard_map/all_to_all | solution.py:63
  85.7 1.0 reduce.1
  87.1 0.3 fusion.42
  89.6 0.5 while.27
  90.2 0.8 copy.41
  90.9 3.4 %all-to-all-start.3 = ((f32[1,128,256]{1,0,2:T(1,128)}), f32[1,128,256]{1,0,2:T(1,128)S(1)}, u32[]{:S(2)}, u32[]{:S(2)}) async-start(f32[1,128,256]{1,0,2:T(1,128)} %copy.41), calls=%async_computation.3 | async-start | bytes 262144 | tf_op jit(solution)/shard_map/all_to_all | solution.py:64
  94.4 6.1 %all-to-all-done.3 = f32[1,128,256]{1,0,2:T(1,128)S(1)} async-done(((f32[1,128,256]{1,0,2:T(1,128)}), f32[1,128,256]{1,0,2:T(1,128)S(1)}, u32[]{:S(2)}, u32[]{:S(2)}) %all-to-all-start.3) | async-done | bytes 131104 | tf_op jit(solution)/shard_map/all_to_all | solution.py:64
  101.1 8.9 %all_to_all.78 = bf16[8,128,32]{1,2,0:T(8,128)(2,1)S(1)} all-to-all(bf16[8,128,32]{1,2,0:T(8,128)(2,1)S(1)} %concatenate.68), channel_id=1, replica_groups=mesh['tm'=8,'rows'=4] {'tm'}, dimensions={0} | all-to-all | bytes 131072 | tf_op jit(solution)/shard_map/all_to_all | solution.py:68
  110.6 4.9 %collective-permute-start.6 = (bf16[4,1,32,256]{3,2,1,0:T(8,128)(2,1)S(1)}, bf16[4,1,32,256]{3,2,1,0:T(8,128)(2,1)S(1)}, u32[]{:S(2)}, u32[]{:S(2)}) collective-permute-start(bf16[4,1,32,256]{3,2,1,0:T(8,128)(2,1)S(1)} %get-tuple-element.151), channel_id=1, source_target_pairs={{0,1},{1,2},{2,3},{4,5},{5,6},{6,7},{8,9},{9,10},{10,11},{12,13},{... | collective-permute-start | bytes 196616 | tf_op jit(solution)/shard_map/ppermute | solution.py:17
  115.5 1.9 %collective-permute-start.7 = (bf16[4,1,32,256]{3,2,1,0:T(8,128)(2,1)S(1)}, bf16[4,1,32,256]{3,2,1,0:T(8,128)(2,1)S(1)}, u32[]{:S(2)}, u32[]{:S(2)}) collective-permute-start(bf16[4,1,32,256]{3,2,1,0:T(8,128)(2,1)S(1)} %get-tuple-element.152), channel_id=1, source_target_pairs={{1,0},{2,1},{3,2},{5,4},{6,5},{7,6},{9,8},{10,9},{11,10},{13,12},{... | collective-permute-start | bytes 196616 | tf_op jit(solution)/shard_map/ppermute | solution.py:19
  117.5 3.6 %collective-permute-done.7 = bf16[4,1,32,256]{3,2,1,0:T(8,128)(2,1)S(1)} collective-permute-done((bf16[4,1,32,256]{3,2,1,0:T(8,128)(2,1)S(1)}, bf16[4,1,32,256]{3,2,1,0:T(8,128)(2,1)S(1)}, u32[]{:S(2)}, u32[]{:S(2)}) %collective-permute-start.7) | collective-permute-done | bytes 65568 | tf_op jit(solution)/shard_map/ppermute | solution.py:19
  121.3 0.3 fusion.41
  123.8 0.9 fusion.22
  (147 shorter events, 12.1 us)
Async XLA Ops:
  0.9 21.8 %collective-permute-start = (bf16[4,1,32,256]{3,2,1,0:T(8,128)(2,1)S(1)}, bf16[4,1,32,256]{3,2,1,0:T(8,128)(2,1)S(1)}, u32[]{:S(2)}, u32[]{:S(2)}) collective-permute-start(bf16[4,1,32,256]{3,2,1,0:T(8,128)(2,1)S(1)} %get-tuple-element.163), channel_id=1, source_target_pairs={{0,1},{1,2},{2,3},{4,5},{5,6},{6,7},{8,9},{9,10},{10,11},{12,13},{... | collective-permute-start | bytes 196616 | tf_op jit(solution)/shard_map/ppermute | solution.py:17
  5.4 17.2 %collective-permute-start.1 = (bf16[4,1,32,256]{3,2,1,0:T(8,128)(2,1)S(1)}, bf16[4,1,32,256]{3,2,1,0:T(8,128)(2,1)S(1)}, u32[]{:S(2)}, u32[]{:S(2)}) collective-permute-start(bf16[4,1,32,256]{3,2,1,0:T(8,128)(2,1)S(1)} %get-tuple-element.164), channel_id=1, source_target_pairs={{1,0},{2,1},{3,2},{5,4},{6,5},{7,6},{9,8},{10,9},{11,10},{13,12},{... | collective-permute-start | bytes 196616 | tf_op jit(solution)/shard_map/ppermute | solution.py:19
  9.7 11.7 %all-to-all-start.1 = ((f32[1,1,256]{1,0,2:T(1,128)}), f32[1,1,256]{1,0,2:T(1,128)S(1)}, u32[]{:S(2)}, u32[]{:S(2)}) async-start(f32[1,1,256]{1,0,2:T(1,128)} %copy.39), calls=%async_computation.1 | async-start | bytes 262144 | tf_op jit(solution)/shard_map/all_to_all | solution.py:63
  15.2 7.4 %copy-start = (bf16[4,4,32,256]{3,2,1,0:T(8,128)(2,1)S(1)}, bf16[4,4,32,256]{3,2,1,0:T(8,128)(2,1)}, u32[]{:S(2)}) copy-start(bf16[4,4,32,256]{3,2,1,0:T(8,128)(2,1)} %param.10) | copy-start | bytes 786436
  31.0 10.6 %all-to-all-start = ((f32[1,128,256]{1,0,2:T(1,128)}), f32[1,128,256]{1,0,2:T(1,128)S(1)}, u32[]{:S(2)}, u32[]{:S(2)}) async-start(f32[1,128,256]{1,0,2:T(1,128)} %copy.37), calls=%async_computation | async-start | bytes 262144 | tf_op jit(solution)/shard_map/all_to_all | solution.py:64
  42.9 9.1 %all-to-all-start.2 = ((bf16[8,128,32]{1,2,0:T(8,128)(2,1)}), bf16[8,128,32]{1,2,0:T(8,128)(2,1)S(1)}, u32[]{:S(2)}, u32[]{:S(2)}) async-start(bf16[8,128,32]{1,2,0:T(8,128)(2,1)} %concatenate.59), calls=%async_computation.2 | async-start | bytes 131072 | tf_op jit(solution)/shard_map/all_to_all | solution.py:68
  52.0 10.6 %copy-start.2 = (f32[2,256]{1,0:T(2,128)S(1)}, f32[2,256]{1,0:T(2,128)}, u32[]{:S(2)}) copy-start(f32[2,256]{1,0:T(2,128)} %param.15) | copy-start | bytes 6148
  54.4 8.2 %collective-permute-start.2 = (bf16[4,1,32,256]{3,2,1,0:T(8,128)(2,1)S(1)}, bf16[4,1,32,256]{3,2,1,0:T(8,128)(2,1)S(1)}, u32[]{:S(2)}, u32[]{:S(2)}) collective-permute-start(bf16[4,1,32,256]{3,2,1,0:T(8,128)(2,1)S(1)} %get-tuple-element.159), channel_id=1, source_target_pairs={{0,1},{1,2},{2,3},{4,5},{5,6},{6,7},{8,9},{9,10},{10,11},{12,13},{... | collective-permute-start | bytes 196616 | tf_op jit(solution)/shard_map/ppermute | solution.py:17
  60.7 5.6 %collective-permute-start.3 = (bf16[4,1,32,256]{3,2,1,0:T(8,128)(2,1)S(1)}, bf16[4,1,32,256]{3,2,1,0:T(8,128)(2,1)S(1)}, u32[]{:S(2)}, u32[]{:S(2)}) collective-permute-start(bf16[4,1,32,256]{3,2,1,0:T(8,128)(2,1)S(1)} %get-tuple-element.160), channel_id=1, source_target_pairs={{1,0},{2,1},{3,2},{5,4},{6,5},{7,6},{9,8},{10,9},{11,10},{13,12},{... | collective-permute-start | bytes 196616 | tf_op jit(solution)/shard_map/ppermute | solution.py:19
  66.5 1.3 %copy-start.1 = (bf16[3,3,256,256]{3,2,1,0:T(8,128)(2,1)S(1)}, bf16[3,3,256,256]{3,2,1,0:T(8,128)(2,1)}, u32[]{:S(2)}) copy-start(bf16[3,3,256,256]{3,2,1,0:T(8,128)(2,1)} %get-tuple-element.122) | copy-start | bytes 3538948
  70.1 16.8 %collective-permute-start.4 = (bf16[4,1,32,256]{3,2,1,0:T(8,128)(2,1)S(1)}, bf16[4,1,32,256]{3,2,1,0:T(8,128)(2,1)S(1)}, u32[]{:S(2)}, u32[]{:S(2)}) collective-permute-start(bf16[4,1,32,256]{3,2,1,0:T(8,128)(2,1)S(1)} %get-tuple-element.155), channel_id=1, source_target_pairs={{0,1},{1,2},{2,3},{4,5},{5,6},{6,7},{8,9},{9,10},{10,11},{12,13},{... | collective-permute-start | bytes 196616 | tf_op jit(solution)/shard_map/ppermute | solution.py:17
  72.0 14.8 %collective-permute-start.5 = (bf16[4,1,32,256]{3,2,1,0:T(8,128)(2,1)S(1)}, bf16[4,1,32,256]{3,2,1,0:T(8,128)(2,1)S(1)}, u32[]{:S(2)}, u32[]{:S(2)}) collective-permute-start(bf16[4,1,32,256]{3,2,1,0:T(8,128)(2,1)S(1)} %get-tuple-element.156), channel_id=1, source_target_pairs={{1,0},{2,1},{3,2},{5,4},{6,5},{7,6},{9,8},{10,9},{11,10},{13,12},{... | collective-permute-start | bytes 196616 | tf_op jit(solution)/shard_map/ppermute | solution.py:19
  75.3 10.4 %all-to-all-start.4 = ((f32[1,1,256]{1,0,2:T(1,128)}), f32[1,1,256]{1,0,2:T(1,128)S(1)}, u32[]{:S(2)}, u32[]{:S(2)}) async-start(f32[1,1,256]{1,0,2:T(1,128)} %copy.43), calls=%async_computation.4 | async-start | bytes 262144 | tf_op jit(solution)/shard_map/all_to_all | solution.py:63
  90.9 9.6 %all-to-all-start.3 = ((f32[1,128,256]{1,0,2:T(1,128)}), f32[1,128,256]{1,0,2:T(1,128)S(1)}, u32[]{:S(2)}, u32[]{:S(2)}) async-start(f32[1,128,256]{1,0,2:T(1,128)} %copy.41), calls=%async_computation.3 | async-start | bytes 262144 | tf_op jit(solution)/shard_map/all_to_all | solution.py:64
  110.6 6.8 %collective-permute-start.6 = (bf16[4,1,32,256]{3,2,1,0:T(8,128)(2,1)S(1)}, bf16[4,1,32,256]{3,2,1,0:T(8,128)(2,1)S(1)}, u32[]{:S(2)}, u32[]{:S(2)}) collective-permute-start(bf16[4,1,32,256]{3,2,1,0:T(8,128)(2,1)S(1)} %get-tuple-element.151), channel_id=1, source_target_pairs={{0,1},{1,2},{2,3},{4,5},{5,6},{6,7},{8,9},{9,10},{10,11},{12,13},{... | collective-permute-start | bytes 196616 | tf_op jit(solution)/shard_map/ppermute | solution.py:17
  115.5 5.6 %collective-permute-start.7 = (bf16[4,1,32,256]{3,2,1,0:T(8,128)(2,1)S(1)}, bf16[4,1,32,256]{3,2,1,0:T(8,128)(2,1)S(1)}, u32[]{:S(2)}, u32[]{:S(2)}) collective-permute-start(bf16[4,1,32,256]{3,2,1,0:T(8,128)(2,1)S(1)} %get-tuple-element.152), channel_id=1, source_target_pairs={{1,0},{2,1},{3,2},{5,4},{6,5},{7,6},{9,8},{10,9},{11,10},{13,12},{... | collective-permute-start | bytes 196616 | tf_op jit(solution)/shard_map/ppermute | solution.py:19
where the time goes:
time: 126 us; the launch traced here: 125 us
  starting transfers between devices  44.8 us (36%)
  waiting for transfers between devices  34.8 us (28%)
  local copies, waits for them, and re-layouts  15.8 us (13%)
  other arithmetic  10.4 us (8%)
  blocking collectives  8.91 us (7%)
  matrix products  8.88 us (7%)
    ppermute x4, starting transfers between devices, extended(): lax.ppermute(tail, axis, [(i, (i + 1) % count) for i in range(ends)])  17.6 us
    all_to_all x2, waiting for transfers between devices, carried_in(): lax.all_to_all(flat_state, 'tm', split_axis=2, concat_axis=0, tiled=True)  13.4 us
    all_to_all x2, waiting for transfers between devices, carried_in(): lax.all_to_all(flattened_decay, 'tm', split_axis=2, concat_axis=0, tiled=...  11.3 us
    all_to_all x1, blocking collectives, carried_in(): lax.all_to_all(exclusive.astype(jnp.bfloat16), 'tm', split_axis=0, concat...  8.91 us
    all_to_all x2, starting transfers between devices, carried_in(): lax.all_to_all(flattened_decay, 'tm', split_axis=2, concat_axis=0, tiled=...  8.9 us
    dot_general x36, matrix products, convolve(): jnp.dot(window, kernel[row_tap, col_tap], preferred_element_type=jnp.floa...  8.88 us
    ppermute x4, starting transfers between devices, extended(): lax.ppermute(head, axis, [((i + 1) % count, i) for i in range(ends)])  8.17 us
    ppermute x4, waiting for transfers between devices, extended(): lax.ppermute(head, axis, [((i + 1) % count, i) for i in range(ends)])  7.24 us
  transfers between devices with their start and end apart: 13, of which 7 were waited for; matrix products, arithmetic and copies ran while one was open for 8% of the time, Pallas kernels for 0%

commit v1 on v0

--- a/solution.py
+++ b/solution.py
@@ -61,7 +61,12 @@
     flattened_decay = segment_attenuation.reshape(1, 1, channels)
     spread_decay, spread_state = (
         lax.all_to_all(flattened_decay, "tm", split_axis=2, concat_axis=0, tiled=True),
-        lax.all_to_all(flat_state, "tm", split_axis=2, concat_axis=0, tiled=True),
+        jnp.concatenate(
+            lax.all_to_all(
+                jnp.stack(jnp.split(flat_state, lax.axis_size("tm"), axis=2)), "tm", 0, 0
+            ),
+            axis=0,
+        ),
     )
     _, inclusive = lax.associative_scan(combine, (spread_decay, spread_state), axis=0)
     exclusive = jnp.concatenate([jnp.zeros_like(inclusive[:1]), inclusive[:-1]], axis=0)

time: 126 us -> 136 us (1.079)
  local copies, waits for them, and re-layouts: 15.8 us -> 25.6 us
    unnamed x8 -> x22, local copies, waits for them, and re-layouts: 1.05 us -> 9.65 us
    another operation x4 -> x22, local copies, waits for them, and re-layouts: 1.6 us -> 2.73 us  [the longest x20 2.65 us: carried_in(): jnp.stack(jnp.split(flat_state, lax.axis_size('tm'), axis=2))]
where the time goes in v1:
time: 136 us; the launch traced here: 135 us
  starting transfers between devices  44.8 us (33%)
  waiting for transfers between devices  34.8 us (26%)
  local copies, waits for them, and re-layouts  25.6 us (19%)
  other arithmetic  10.4 us (8%)
  blocking collectives  8.92 us (7%)
  matrix products  8.89 us (7%)
    ppermute x4, starting transfers between devices, extended(): lax.ppermute(tail, axis, [(i, (i + 1) % count) for i in range(ends)])  17.6 us
    all_to_all x2, waiting for transfers between devices, carried_in(): lax.all_to_all(jnp.stack(jnp.split(flat_state, lax.axis_size('tm'), axis=...  13.4 us
    all_to_all x2, waiting for transfers between devices, carried_in(): lax.all_to_all(flattened_decay, 'tm', split_axis=2, concat_axis=0, tiled=...  11.3 us
    unnamed x22, local copies, waits for them, and re-layouts  9.65 us
    all_to_all x1, blocking collectives, carried_in(): lax.all_to_all(exclusive.astype(jnp.bfloat16), 'tm', split_axis=0, concat...  8.92 us
    all_to_all x2, starting transfers between devices, carried_in(): lax.all_to_all(flattened_decay, 'tm', split_axis=2, concat_axis=0, tiled=...  8.9 us
    dot_general x36, matrix products, convolve(): jnp.dot(window, kernel[row_tap, col_tap], preferred_element_type=jnp.floa...  8.89 us
    ppermute x4, starting transfers between devices, extended(): lax.ppermute(head, axis, [((i + 1) % count, i) for i in range(ends)])  8.17 us
  transfers between devices with their start and end apart: 13, of which 7 were waited for; matrix products, arithmetic and copies ran while one was open for 8% of the time, Pallas kernels for 0%

profile of v1, /device:TPU:1, one launch (start us, length us, event | category | flops | bytes accessed | tf_op | source)
XLA Modules:
  0.0 134.5 jit_solution(10853857078694607525)
XLA Ops:
  0.0 0.9 fusion.48
  0.9 4.5 %collective-permute-start = (bf16[4,1,32,256]{3,2,1,0:T(8,128)(2,1)S(1)}, bf16[4,1,32,256]{3,2,1,0:T(8,128)(2,1)S(1)}, u32[]{:S(2)}, u32[]{:S(2)}) collective-permute-start(bf16[4,1,32,256]{3,2,1,0:T(8,128)(2,1)S(1)} %get-tuple-element.163), channel_id=1, source_target_pairs={{0,1},{1,2},{2,3},{4,5},{5,6},{6,7},{8,9},{9,10},{10,11},{12,13},{... | collective-permute-start | bytes 196616 | tf_op jit(solution)/shard_map/ppermute | solution.py:17
  5.4 1.9 %collective-permute-start.1 = (bf16[4,1,32,256]{3,2,1,0:T(8,128)(2,1)S(1)}, bf16[4,1,32,256]{3,2,1,0:T(8,128)(2,1)S(1)}, u32[]{:S(2)}, u32[]{:S(2)}) collective-permute-start(bf16[4,1,32,256]{3,2,1,0:T(8,128)(2,1)S(1)} %get-tuple-element.164), channel_id=1, source_target_pairs={{1,0},{2,1},{3,2},{5,4},{6,5},{7,6},{9,8},{10,9},{11,10},{13,12},{... | collective-permute-start | bytes 196616 | tf_op jit(solution)/shard_map/ppermute | solution.py:19
  7.3 0.8 fusion.52
  8.1 0.7 neg.5
  8.9 0.8 copy.31
  9.7 5.5 %all-to-all-start.1 = ((f32[1,1,256]{1,0,2:T(1,128)}), f32[1,1,256]{1,0,2:T(1,128)S(1)}, u32[]{:S(2)}, u32[]{:S(2)}) async-start(f32[1,1,256]{1,0,2:T(1,128)} %copy.31), calls=%async_computation.1 | async-start | bytes 262144 | tf_op jit(solution)/shard_map/all_to_all | solution.py:63
  15.2 1.9 %slice_bitcast_fusion.1 = (bf16[3,3,256,256]{3,2,1,0:T(8,128)(2,1)S(1)}, bf16[3,3,256,256]{3,2,1,0:T(8,128)(2,1)S(1)}) fusion(bf16[2,3,3,256,256]{4,3,2,1,0:T(8,128)(2,1)} %param.13), kind=kLoop, calls=%fused_computation.47 | loop fusion | bytes 4718592 | tf_op jit(solution)/shard_map/squeeze | solution.py:85
  17.1 4.3 %all-to-all-done.1 = f32[1,1,256]{1,0,2:T(1,128)S(1)} async-done(((f32[1,1,256]{1,0,2:T(1,128)}), f32[1,1,256]{1,0,2:T(1,128)S(1)}, u32[]{:S(2)}, u32[]{:S(2)}) %all-to-all-start.1) | async-done | bytes 1056 | tf_op jit(solution)/shard_map/all_to_all | solution.py:63
  21.4 1.0 reduce
  25.1 1.0 fusion.5
  26.2 4.1 %while.26 = (s32[]{:T(128)}, f32[4,32,256]{2,1,0:T(8,128)S(1)}, f32[4,4,32,256]{3,2,1,0:T(8,128)S(1)}, f32[4,256]{1,0:T(4,128)S(1)}, f32[4,4,32,256]{3,2,1,0:T(8,128)}, /*index=5*/s32[]{:T(128)}, s32[]{:T(128)}) while((s32[]{:T(128)}, f32[4,32,256]{2,1,0:T(8,128)S(1)}, f32[4,4,32,256]{3,2,1,0:T(8,128)S(1)}, ...), condition=%wide.region_1.2_spmd.clone, body=%wide.region_0.1_spmd.clone.sunk | while | flops 131587 | bytes 530527 | solution.py:50
  26.2 1.0 bitcast_dynamic-update-slice_fusion.4
  27.2 1.0 bitcast_dynamic-update-slice_fusion.4
  28.3 1.0 bitcast_dynamic-update-slice_fusion.4
  29.3 1.0 bitcast_dynamic-update-slice_fusion.4
  30.5 0.6 constant_dynamic-update-slice_fusion.7
  31.6 0.6 constant_dynamic-update-slice_fusion.6
  32.3 0.6 constant_dynamic-update-slice_fusion.5
  32.9 0.6 constant_dynamic-update-slice_fusion.4
  33.5 0.6 constant_dynamic-update-slice_fusion.3
  35.9 3.4 %all-to-all-start = ((f32[8,1,128,32]{2,3,1,0:T(8,128)}), f32[8,1,128,32]{2,3,1,0:T(8,128)S(1)}, u32[]{:S(2)}, u32[]{:S(2)}) async-start(f32[8,1,128,32]{2,3,1,0:T(8,128)} %constant_dynamic-update-slice_fusion), calls=%async_computation | async-start | bytes 262144 | tf_op jit(solution)/shard_map/all_to_all | solution.py:65
  39.3 7.2 %all-to-all-done = f32[8,1,128,32]{2,3,1,0:T(8,128)S(1)} async-done(((f32[8,1,128,32]{2,3,1,0:T(8,128)}), f32[8,1,128,32]{2,3,1,0:T(8,128)S(1)}, u32[]{:S(2)}, u32[]{:S(2)}) %all-to-all-start) | async-done | bytes 131104 | tf_op jit(solution)/shard_map/all_to_all | solution.py:65
  47.2 0.6 concatenate.59
  47.8 3.4 %all-to-all-start.2 = ((bf16[8,128,32]{1,2,0:T(8,128)(2,1)}), bf16[8,128,32]{1,2,0:T(8,128)(2,1)S(1)}, u32[]{:S(2)}, u32[]{:S(2)}) async-start(bf16[8,128,32]{1,2,0:T(8,128)(2,1)} %concatenate.59), calls=%async_computation.2 | async-start | bytes 131072 | tf_op jit(solution)/shard_map/all_to_all | solution.py:73
  51.2 2.9 %slice_bitcast_fusion = (bf16[3,3,256,256]{3,2,1,0:T(8,128)(2,1)S(1)}, bf16[3,3,256,256]{3,2,1,0:T(8,128)(2,1)}) fusion(bf16[2,3,3,256,256]{4,3,2,1,0:T(8,128)(2,1)} %param.14), kind=kLoop, calls=%fused_computation.46 | loop fusion | bytes 4718592 | tf_op jit(solution)/shard_map/squeeze | solution.py:91
  54.1 2.8 %all-to-all-done.2 = bf16[8,128,32]{1,2,0:T(8,128)(2,1)S(1)} async-done(((bf16[8,128,32]{1,2,0:T(8,128)(2,1)}), bf16[8,128,32]{1,2,0:T(8,128)(2,1)S(1)}, u32[]{:S(2)}, u32[]{:S(2)}) %all-to-all-start.2) | async-done | bytes 65568 | tf_op jit(solution)/shard_map/all_to_all | solution.py:73
  56.9 1.1 reshape.236
  58.0 1.2 copy.43
  59.3 6.2 %collective-permute-start.2 = (bf16[4,1,32,256]{3,2,1,0:T(8,128)(2,1)S(1)}, bf16[4,1,32,256]{3,2,1,0:T(8,128)(2,1)S(1)}, u32[]{:S(2)}, u32[]{:S(2)}) collective-permute-start(bf16[4,1,32,256]{3,2,1,0:T(8,128)(2,1)S(1)} %get-tuple-element.159), channel_id=1, source_target_pairs={{0,1},{1,2},{2,3},{4,5},{5,6},{6,7},{8,9},{9,10},{10,11},{12,13},{... | collective-permute-start | bytes 196616 | tf_op jit(solution)/shard_map/ppermute | solution.py:17
  65.6 1.9 %collective-permute-start.3 = (bf16[4,1,32,256]{3,2,1,0:T(8,128)(2,1)S(1)}, bf16[4,1,32,256]{3,2,1,0:T(8,128)(2,1)S(1)}, u32[]{:S(2)}, u32[]{:S(2)}) collective-permute-start(bf16[4,1,32,256]{3,2,1,0:T(8,128)(2,1)S(1)} %get-tuple-element.160), channel_id=1, source_target_pairs={{1,0},{2,1},{3,2},{5,4},{6,5},{7,6},{9,8},{10,9},{11,10},{13,12},{... | collective-permute-start | bytes 196616 | tf_op jit(solution)/shard_map/ppermute | solution.py:19
  67.6 3.6 %collective-permute-done.3 = bf16[4,1,32,256]{3,2,1,0:T(8,128)(2,1)S(1)} collective-permute-done((bf16[4,1,32,256]{3,2,1,0:T(8,128)(2,1)S(1)}, bf16[4,1,32,256]{3,2,1,0:T(8,128)(2,1)S(1)}, u32[]{:S(2)}, u32[]{:S(2)}) %collective-permute-start.3) | collective-permute-done | bytes 65568 | tf_op jit(solution)/shard_map/ppermute | solution.py:19
  71.7 1.0 copy-done.1
  75.0 1.9 %collective-permute-start.4 = (bf16[4,1,32,256]{3,2,1,0:T(8,128)(2,1)S(1)}, bf16[4,1,32,256]{3,2,1,0:T(8,128)(2,1)S(1)}, u32[]{:S(2)}, u32[]{:S(2)}) collective-permute-start(bf16[4,1,32,256]{3,2,1,0:T(8,128)(2,1)S(1)} %get-tuple-element.155), channel_id=1, source_target_pairs={{0,1},{1,2},{2,3},{4,5},{5,6},{6,7},{8,9},{9,10},{10,11},{12,13},{... | collective-permute-start | bytes 196616 | tf_op jit(solution)/shard_map/ppermute | solution.py:17
  77.0 2.4 %collective-permute-start.5 = (bf16[4,1,32,256]{3,2,1,0:T(8,128)(2,1)S(1)}, bf16[4,1,32,256]{3,2,1,0:T(8,128)(2,1)S(1)}, u32[]{:S(2)}, u32[]{:S(2)}) collective-permute-start(bf16[4,1,32,256]{3,2,1,0:T(8,128)(2,1)S(1)} %get-tuple-element.156), channel_id=1, source_target_pairs={{1,0},{2,1},{3,2},{5,4},{6,5},{7,6},{9,8},{10,9},{11,10},{13,12},{... | collective-permute-start | bytes 196616 | tf_op jit(solution)/shard_map/ppermute | solution.py:19
  79.4 0.8 copy.41
  80.2 3.4 %all-to-all-start.4 = ((f32[1,1,256]{1,0,2:T(1,128)}), f32[1,1,256]{1,0,2:T(1,128)S(1)}, u32[]{:S(2)}, u32[]{:S(2)}) async-start(f32[1,1,256]{1,0,2:T(1,128)} %copy.41), calls=%async_computation.4 | async-start | bytes 262144 | tf_op jit(solution)/shard_map/all_to_all | solution.py:63
  83.6 7.0 %all-to-all-done.4 = f32[1,1,256]{1,0,2:T(1,128)S(1)} async-done(((f32[1,1,256]{1,0,2:T(1,128)}), f32[1,1,256]{1,0,2:T(1,128)S(1)}, u32[]{:S(2)}, u32[]{:S(2)}) %all-to-all-start.4) | async-done | bytes 1056 | tf_op jit(solution)/shard_map/all_to_all | solution.py:63
  90.6 1.0 reduce.1
  95.3 0.6 constant_dynamic-update-slice_fusion.15
  96.4 0.6 constant_dynamic-update-slice_fusion.14
  100.7 3.4 %all-to-all-start.3 = ((f32[8,1,128,32]{2,3,1,0:T(8,128)}), f32[8,1,128,32]{2,3,1,0:T(8,128)S(1)}, u32[]{:S(2)}, u32[]{:S(2)}) async-start(f32[8,1,128,32]{2,3,1,0:T(8,128)} %constant_dynamic-update-slice_fusion.8), calls=%async_computation.3 | async-start | bytes 262144 | tf_op jit(solution)/shard_map/all_to_all | solution.py:65
  104.1 6.1 %all-to-all-done.3 = f32[8,1,128,32]{2,3,1,0:T(8,128)S(1)} async-done(((f32[8,1,128,32]{2,3,1,0:T(8,128)}), f32[8,1,128,32]{2,3,1,0:T(8,128)S(1)}, u32[]{:S(2)}, u32[]{:S(2)}) %all-to-all-start.3) | async-done | bytes 131104 | tf_op jit(solution)/shard_map/all_to_all | solution.py:65
  110.9 8.9 %all_to_all.52 = bf16[8,128,32]{1,2,0:T(8,128)(2,1)S(1)} all-to-all(bf16[8,128,32]{1,2,0:T(8,128)(2,1)S(1)} %concatenate.68), channel_id=1, replica_groups=mesh['tm'=8,'rows'=4] {'tm'}, dimensions={0} | all-to-all | bytes 131072 | tf_op jit(solution)/shard_map/all_to_all | solution.py:73
  120.4 4.9 %collective-permute-start.6 = (bf16[4,1,32,256]{3,2,1,0:T(8,128)(2,1)S(1)}, bf16[4,1,32,256]{3,2,1,0:T(8,128)(2,1)S(1)}, u32[]{:S(2)}, u32[]{:S(2)}) collective-permute-start(bf16[4,1,32,256]{3,2,1,0:T(8,128)(2,1)S(1)} %get-tuple-element.151), channel_id=1, source_target_pairs={{0,1},{1,2},{2,3},{4,5},{5,6},{6,7},{8,9},{9,10},{10,11},{12,13},{... | collective-permute-start | bytes 196616 | tf_op jit(solution)/shard_map/ppermute | solution.py:17
  125.3 1.9 %collective-permute-start.7 = (bf16[4,1,32,256]{3,2,1,0:T(8,128)(2,1)S(1)}, bf16[4,1,32,256]{3,2,1,0:T(8,128)(2,1)S(1)}, u32[]{:S(2)}, u32[]{:S(2)}) collective-permute-start(bf16[4,1,32,256]{3,2,1,0:T(8,128)(2,1)S(1)} %get-tuple-element.152), channel_id=1, source_target_pairs={{1,0},{2,1},{3,2},{5,4},{6,5},{7,6},{9,8},{10,9},{11,10},{13,12},{... | collective-permute-start | bytes 196616 | tf_op jit(solution)/shard_map/ppermute | solution.py:19
  127.3 3.6 %collective-permute-done.7 = bf16[4,1,32,256]{3,2,1,0:T(8,128)(2,1)S(1)} collective-permute-done((bf16[4,1,32,256]{3,2,1,0:T(8,128)(2,1)S(1)}, bf16[4,1,32,256]{3,2,1,0:T(8,128)(2,1)S(1)}, u32[]{:S(2)}, u32[]{:S(2)}) %collective-permute-start.7) | collective-permute-done | bytes 65568 | tf_op jit(solution)/shard_map/ppermute | solution.py:19
  133.6 0.9 fusion.22
  (179 shorter events, 20.7 us)
Async XLA Ops:
  0.9 21.8 %collective-permute-start = (bf16[4,1,32,256]{3,2,1,0:T(8,128)(2,1)S(1)}, bf16[4,1,32,256]{3,2,1,0:T(8,128)(2,1)S(1)}, u32[]{:S(2)}, u32[]{:S(2)}) collective-permute-start(bf16[4,1,32,256]{3,2,1,0:T(8,128)(2,1)S(1)} %get-tuple-element.163), channel_id=1, source_target_pairs={{0,1},{1,2},{2,3},{4,5},{5,6},{6,7},{8,9},{9,10},{10,11},{12,13},{... | collective-permute-start | bytes 196616 | tf_op jit(solution)/shard_map/ppermute | solution.py:17
  5.4 17.2 %collective-permute-start.1 = (bf16[4,1,32,256]{3,2,1,0:T(8,128)(2,1)S(1)}, bf16[4,1,32,256]{3,2,1,0:T(8,128)(2,1)S(1)}, u32[]{:S(2)}, u32[]{:S(2)}) collective-permute-start(bf16[4,1,32,256]{3,2,1,0:T(8,128)(2,1)S(1)} %get-tuple-element.164), channel_id=1, source_target_pairs={{1,0},{2,1},{3,2},{5,4},{6,5},{7,6},{9,8},{10,9},{11,10},{13,12},{... | collective-permute-start | bytes 196616 | tf_op jit(solution)/shard_map/ppermute | solution.py:19
  9.7 11.7 %all-to-all-start.1 = ((f32[1,1,256]{1,0,2:T(1,128)}), f32[1,1,256]{1,0,2:T(1,128)S(1)}, u32[]{:S(2)}, u32[]{:S(2)}) async-start(f32[1,1,256]{1,0,2:T(1,128)} %copy.31), calls=%async_computation.1 | async-start | bytes 262144 | tf_op jit(solution)/shard_map/all_to_all | solution.py:63
  15.2 7.4 %copy-start = (bf16[4,4,32,256]{3,2,1,0:T(8,128)(2,1)S(1)}, bf16[4,4,32,256]{3,2,1,0:T(8,128)(2,1)}, u32[]{:S(2)}) copy-start(bf16[4,4,32,256]{3,2,1,0:T(8,128)(2,1)} %param.10) | copy-start | bytes 786436
  35.9 10.6 %all-to-all-start = ((f32[8,1,128,32]{2,3,1,0:T(8,128)}), f32[8,1,128,32]{2,3,1,0:T(8,128)S(1)}, u32[]{:S(2)}, u32[]{:S(2)}) async-start(f32[8,1,128,32]{2,3,1,0:T(8,128)} %constant_dynamic-update-slice_fusion), calls=%async_computation | async-start | bytes 262144 | tf_op jit(solution)/shard_map/all_to_all | solution.py:65
  47.8 9.1 %all-to-all-start.2 = ((bf16[8,128,32]{1,2,0:T(8,128)(2,1)}), bf16[8,128,32]{1,2,0:T(8,128)(2,1)S(1)}, u32[]{:S(2)}, u32[]{:S(2)}) async-start(bf16[8,128,32]{1,2,0:T(8,128)(2,1)} %concatenate.59), calls=%async_computation.2 | async-start | bytes 131072 | tf_op jit(solution)/shard_map/all_to_all | solution.py:73
  56.9 10.6 %copy-start.2 = (f32[2,256]{1,0:T(2,128)S(1)}, f32[2,256]{1,0:T(2,128)}, u32[]{:S(2)}) copy-start(f32[2,256]{1,0:T(2,128)} %param.15) | copy-start | bytes 6148
  59.3 8.2 %collective-permute-start.2 = (bf16[4,1,32,256]{3,2,1,0:T(8,128)(2,1)S(1)}, bf16[4,1,32,256]{3,2,1,0:T(8,128)(2,1)S(1)}, u32[]{:S(2)}, u32[]{:S(2)}) collective-permute-start(bf16[4,1,32,256]{3,2,1,0:T(8,128)(2,1)S(1)} %get-tuple-element.159), channel_id=1, source_target_pairs={{0,1},{1,2},{2,3},{4,5},{5,6},{6,7},{8,9},{9,10},{10,11},{12,13},{... | collective-permute-start | bytes 196616 | tf_op jit(solution)/shard_map/ppermute | solution.py:17
  65.6 5.6 %collective-permute-start.3 = (bf16[4,1,32,256]{3,2,1,0:T(8,128)(2,1)S(1)}, bf16[4,1,32,256]{3,2,1,0:T(8,128)(2,1)S(1)}, u32[]{:S(2)}, u32[]{:S(2)}) collective-permute-start(bf16[4,1,32,256]{3,2,1,0:T(8,128)(2,1)S(1)} %get-tuple-element.160), channel_id=1, source_target_pairs={{1,0},{2,1},{3,2},{5,4},{6,5},{7,6},{9,8},{10,9},{11,10},{13,12},{... | collective-permute-start | bytes 196616 | tf_op jit(solution)/shard_map/ppermute | solution.py:19
  71.4 1.3 copy-start.1
  75.0 16.8 %collective-permute-start.4 = (bf16[4,1,32,256]{3,2,1,0:T(8,128)(2,1)S(1)}, bf16[4,1,32,256]{3,2,1,0:T(8,128)(2,1)S(1)}, u32[]{:S(2)}, u32[]{:S(2)}) collective-permute-start(bf16[4,1,32,256]{3,2,1,0:T(8,128)(2,1)S(1)} %get-tuple-element.155), channel_id=1, source_target_pairs={{0,1},{1,2},{2,3},{4,5},{5,6},{6,7},{8,9},{9,10},{10,11},{12,13},{... | collective-permute-start | bytes 196616 | tf_op jit(solution)/shard_map/ppermute | solution.py:17
  77.0 14.8 %collective-permute-start.5 = (bf16[4,1,32,256]{3,2,1,0:T(8,128)(2,1)S(1)}, bf16[4,1,32,256]{3,2,1,0:T(8,128)(2,1)S(1)}, u32[]{:S(2)}, u32[]{:S(2)}) collective-permute-start(bf16[4,1,32,256]{3,2,1,0:T(8,128)(2,1)S(1)} %get-tuple-element.156), channel_id=1, source_target_pairs={{1,0},{2,1},{3,2},{5,4},{6,5},{7,6},{9,8},{10,9},{11,10},{13,12},{... | collective-permute-start | bytes 196616 | tf_op jit(solution)/shard_map/ppermute | solution.py:19
  80.2 10.4 %all-to-all-start.4 = ((f32[1,1,256]{1,0,2:T(1,128)}), f32[1,1,256]{1,0,2:T(1,128)S(1)}, u32[]{:S(2)}, u32[]{:S(2)}) async-start(f32[1,1,256]{1,0,2:T(1,128)} %copy.41), calls=%async_computation.4 | async-start | bytes 262144 | tf_op jit(solution)/shard_map/all_to_all | solution.py:63
  100.7 9.5 %all-to-all-start.3 = ((f32[8,1,128,32]{2,3,1,0:T(8,128)}), f32[8,1,128,32]{2,3,1,0:T(8,128)S(1)}, u32[]{:S(2)}, u32[]{:S(2)}) async-start(f32[8,1,128,32]{2,3,1,0:T(8,128)} %constant_dynamic-update-slice_fusion.8), calls=%async_computation.3 | async-start | bytes 262144 | tf_op jit(solution)/shard_map/all_to_all | solution.py:65
  120.4 6.9 %collective-permute-start.6 = (bf16[4,1,32,256]{3,2,1,0:T(8,128)(2,1)S(1)}, bf16[4,1,32,256]{3,2,1,0:T(8,128)(2,1)S(1)}, u32[]{:S(2)}, u32[]{:S(2)}) collective-permute-start(bf16[4,1,32,256]{3,2,1,0:T(8,128)(2,1)S(1)} %get-tuple-element.151), channel_id=1, source_target_pairs={{0,1},{1,2},{2,3},{4,5},{5,6},{6,7},{8,9},{9,10},{10,11},{12,13},{... | collective-permute-start | bytes 196616 | tf_op jit(solution)/shard_map/ppermute | solution.py:17
  125.3 5.6 %collective-permute-start.7 = (bf16[4,1,32,256]{3,2,1,0:T(8,128)(2,1)S(1)}, bf16[4,1,32,256]{3,2,1,0:T(8,128)(2,1)S(1)}, u32[]{:S(2)}, u32[]{:S(2)}) collective-permute-start(bf16[4,1,32,256]{3,2,1,0:T(8,128)(2,1)S(1)} %get-tuple-element.152), channel_id=1, source_target_pairs={{1,0},{2,1},{3,2},{5,4},{6,5},{7,6},{9,8},{10,9},{11,10},{13,12},{... | collective-permute-start | bytes 196616 | tf_op jit(solution)/shard_map/ppermute | solution.py:19
